TPU v7x, 32 devices: a whole 2x2x4 slice. The times are simulated.
32 devices in a mesh: seq: 16 (over z, y, x), batch: 2 (over core).
Axes of the slice: x: 2, y: 2, z: 4, core: 2. Of those that a mesh axis runs over, the one named last changes fastest.
Arguments:
- tokens: bfloat16 [2, 2048, 768], P('batch', 'seq'), may hold values from -6 to 6
- cotangent: bfloat16 [2, 2048, 768], P('batch', 'seq'), may hold values from -6 to 6
- prefix_len: int32 [2], P('batch'), may hold values from 204 to 1024
- gain_one: bfloat16 [768], P(('seq', 'batch')), may hold values from 0.25 to 1.75
- shift_one: bfloat16 [768], P(('seq', 'batch')), may hold values from -1.75 to 1.75
- w_query: bfloat16 [768, 768], P(('seq', 'batch')), may hold values from -0.21875 to 0.21875
- b_query: bfloat16 [768], P(('seq', 'batch')), may hold values from -3 to 3
- w_key: bfloat16 [768, 768], P(('seq', 'batch')), may hold values from -0.21875 to 0.21875
- w_value: bfloat16 [768, 768], P(('seq', 'batch')), may hold values from -0.21875 to 0.21875
- b_value: bfloat16 [768], P(('seq', 'batch')), may hold values from -3 to 3
- w_output: bfloat16 [768, 768], P(('seq', 'batch')), may hold values from -3.5 to 3.5
- b_output: bfloat16 [768], P(('seq', 'batch')), may hold values from -1.75 to 1.75
- gain_two: bfloat16 [768], P(('seq', 'batch')), may hold values from 0.25 to 1.75
- shift_two: bfloat16 [768], P(('seq', 'batch')), may hold values from -1.75 to 1.75
- w_up: bfloat16 [768, 3072], P(('seq', 'batch')), may hold values from -0.21875 to 0.21875
- b_up: bfloat16 [3072], P(('seq', 'batch')), may hold values from -3 to 3
- w_down: bfloat16 [3072, 768], P(('seq', 'batch')), may hold values from -0.109375 to 0.109375
- b_down: bfloat16 [768], P(('seq', 'batch')), may hold values from -1.75 to 1.75
Outputs:
- layer_out: bfloat16 [2, 2048, 768], P('batch', 'seq')
- grad_tokens: float32 [2, 2048, 768], P('batch', 'seq')
- grad_gain_one: float32 [768], P(('seq', 'batch'))
- grad_shift_one: float32 [768], P(('seq', 'batch'))
- grad_w_query: float32 [768, 768], P(('seq', 'batch'))
- grad_b_query: float32 [768], P(('seq', 'batch'))
- grad_w_key: float32 [768, 768], P(('seq', 'batch'))
- grad_w_value: float32 [768, 768], P(('seq', 'batch'))
- grad_b_value: float32 [768], P(('seq', 'batch'))
- grad_w_output: float32 [768, 768], P(('seq', 'batch'))
- grad_b_output: float32 [768], P(('seq', 'batch'))
- grad_gain_two: float32 [768], P(('seq', 'batch'))
- grad_shift_two: float32 [768], P(('seq', 'batch'))
- grad_w_up: float32 [768, 3072], P(('seq', 'batch'))
- grad_b_up: float32 [3072], P(('seq', 'batch'))
- grad_w_down: float32 [3072, 768], P(('seq', 'batch'))
- grad_b_down: float32 [768], P(('seq', 'batch'))
Inputs may be any that keep to these rules, and one draw needn't show every extreme that they name: `prefix_len`: one prefix length per sequence.
All inputs are finite; a program needn't handle non-finite values.
Results may differ from a plain program's by a relative error of at most 0.014.
Values may be sent and summed in bfloat16 or wider, within the bound.
No kernel may reach another device: no remote copies, remote signals or barrier semaphores. Data moves between devices by JAX's collectives and lax.ppermute only.
A program may use at most 192 MiB of HBM per device.

v0:
```python
import jax
import jax.numpy as jnp
from jax import lax
from jax.sharding import PartitionSpec as P

HD = 64
EPS = 1e-05


def normalize(values):
    centre = jnp.mean(values, axis=-1, keepdims=True)
    centred = values - centre
    spread = jnp.mean(centred * centred, axis=-1, keepdims=True)
    factor = lax.rsqrt(spread + EPS)
    return (centred * factor, factor)


def norm_backward(grad_out, normed, factor, gain):
    grad_gain = jnp.sum(grad_out * normed, axis=0)
    grad_shift = jnp.sum(grad_out, axis=0)
    scaled = grad_out * gain.astype(jnp.float32)
    grad_in = factor * (
        scaled
        - jnp.mean(scaled, axis=-1, keepdims=True)
        - normed * jnp.mean(scaled * normed, axis=-1, keepdims=True)
    )
    return (grad_in, grad_gain, grad_shift)


def over_rows(left, right):
    return lax.dot_general(
        left, right, (((0,), (0,)), ((), ())), preferred_element_type=jnp.float32
    )


def over_cols(left, right):
    return lax.dot_general(
        left, right, (((1,), (1,)), ((), ())), preferred_element_type=jnp.float32
    )


def pair_scores(q_part, k_part, row_ids, col_ids, prefix):
    scores = jnp.einsum("qhd,khd->hqk", q_part, k_part, preferred_element_type=jnp.float32) * 0.125
    allowed = (col_ids[None, :] <= row_ids[:, None]) | (col_ids[None, :] < prefix)
    return (jnp.where(allowed[None], scores, -1e30), allowed)


def grad_terms(q_part, do_part, lse_part, delta_part, k_part, v_part, row_ids, col_ids, prefix):
    scores, allowed = pair_scores(q_part, k_part, row_ids, col_ids, prefix)
    attn_prob = jnp.where(allowed[None], jnp.exp(scores - lse_part[:, :, None]), 0.0)
    prob_low = attn_prob.astype(jnp.bfloat16)
    d_prob = jnp.einsum("qhd,khd->hqk", do_part, v_part, preferred_element_type=jnp.float32)
    d_score = (attn_prob * (d_prob - delta_part[:, :, None])).astype(jnp.bfloat16)
    return (prob_low, d_score)


def body(
    tokens,
    cotangent,
    prefix_len,
    gain_one,
    shift_one,
    w_query,
    b_query,
    w_key,
    w_value,
    b_value,
    w_output,
    b_output,
    gain_two,
    shift_two,
    w_up,
    b_up,
    w_down,
    b_down,
):
    shards = (
        gain_one,
        shift_one,
        w_query,
        b_query,
        w_key,
        w_value,
        b_value,
        w_output,
        b_output,
        gain_two,
        shift_two,
        w_up,
        b_up,
        w_down,
        b_down,
    )
    gathered = (
        lax.all_gather(shards[0], ("seq", "batch"), axis=0, tiled=True),
        lax.all_gather(shards[1], ("seq", "batch"), axis=0, tiled=True),
        lax.all_gather(shards[2], ("seq", "batch"), axis=0, tiled=True),
        lax.all_gather(shards[3], ("seq", "batch"), axis=0, tiled=True),
        lax.all_gather(shards[4], ("seq", "batch"), axis=0, tiled=True),
        lax.all_gather(shards[5], ("seq", "batch"), axis=0, tiled=True),
        lax.all_gather(shards[6], ("seq", "batch"), axis=0, tiled=True),
        lax.all_gather(shards[7], ("seq", "batch"), axis=0, tiled=True),
        lax.all_gather(shards[8], ("seq", "batch"), axis=0, tiled=True),
        lax.all_gather(shards[9], ("seq", "batch"), axis=0, tiled=True),
        lax.all_gather(shards[10], ("seq", "batch"), axis=0, tiled=True),
        lax.all_gather(shards[11], ("seq", "batch"), axis=0, tiled=True),
        lax.all_gather(shards[12], ("seq", "batch"), axis=0, tiled=True),
        lax.all_gather(shards[13], ("seq", "batch"), axis=0, tiled=True),
        lax.all_gather(shards[14], ("seq", "batch"), axis=0, tiled=True),
    )
    (
        ga_full,
        sa_full,
        wq_full,
        bq_full,
        wk_full,
        wv_full,
        bv_full,
        wo_full,
        bo_full,
        gb_full,
        sb_full,
        wu_full,
        bu_full,
        wd_full,
        bd_full,
    ) = gathered
    hidden = tokens[0].astype(jnp.float32)
    local_rows = hidden.shape[0]
    width = hidden.shape[1]
    heads = width // HD
    prefix = prefix_len[0]
    start_row = lax.axis_index("seq") * local_rows
    last_row = start_row + local_rows - 1
    length = local_rows * lax.axis_size("seq")
    block_rows = min(512, length)
    block_count = length // block_rows
    row_ids = start_row + jnp.arange(local_rows, dtype=jnp.int32)
    block_ids = jnp.arange(block_count, dtype=jnp.int32)
    normed_one, factor_one = normalize(hidden)
    norm_one = (normed_one * ga_full.astype(jnp.float32) + sa_full.astype(jnp.float32)).astype(
        jnp.bfloat16
    )
    q_low = (
        jnp.dot(norm_one, wq_full, preferred_element_type=jnp.float32) + bq_full.astype(jnp.float32)
    ).astype(jnp.bfloat16)
    k_low = jnp.dot(norm_one, wk_full, preferred_element_type=jnp.float32).astype(jnp.bfloat16)
    v_low = (
        jnp.dot(norm_one, wv_full, preferred_element_type=jnp.float32) + bv_full.astype(jnp.float32)
    ).astype(jnp.bfloat16)
    k_all, v_all = (
        lax.all_gather(k_low, "seq", axis=0, tiled=True),
        lax.all_gather(v_low, "seq", axis=0, tiled=True),
    )
    q_heads = q_low.reshape(local_rows, heads, HD)

    def lse_step(state, item):
        k_part, index = item
        col_ids = index * block_rows + jnp.arange(block_rows, dtype=jnp.int32)

        def lse_update(current):
            scores, allowed = pair_scores(q_heads, k_part, row_ids, col_ids, prefix)
            new_top = jnp.maximum(current[0], jnp.max(scores, axis=-1))
            total = current[1] * jnp.exp(current[0] - new_top) + jnp.sum(
                jnp.exp(scores - new_top[:, :, None]), axis=-1
            )
            return (new_top, total)

        needed = (index * block_rows <= last_row) | (index * block_rows < prefix)
        return (lax.cond(needed, lse_update, lambda current: current, state), None)

    k_blocks = k_all.reshape(block_count, block_rows, heads, HD)
    v_blocks = v_all.reshape(block_count, block_rows, heads, HD)
    lse_start = (
        jnp.full((heads, local_rows), -1e30, jnp.float32),
        jnp.zeros((heads, local_rows), jnp.float32),
    )
    (top_all, total_all), _ = lax.scan(lse_step, lse_start, (k_blocks, block_ids))
    lse = top_all + jnp.log(total_all)

    def out_step(acc, item):
        k_part, v_part, index = item
        col_ids = index * block_rows + jnp.arange(block_rows, dtype=jnp.int32)

        def out_update(current):
            scores, allowed = pair_scores(q_heads, k_part, row_ids, col_ids, prefix)
            attn_prob = jnp.where(allowed[None], jnp.exp(scores - lse[:, :, None]), 0.0).astype(
                jnp.bfloat16
            )
            return current + jnp.einsum(
                "hqk,khd->qhd", attn_prob, v_part, preferred_element_type=jnp.float32
            )

        needed = (index * block_rows <= last_row) | (index * block_rows < prefix)
        return (lax.cond(needed, out_update, lambda current: current, acc), None)

    ctx_acc, _ = lax.scan(
        out_step, jnp.zeros((local_rows, heads, HD), jnp.float32), (k_blocks, v_blocks, block_ids)
    )
    ctx_low = ctx_acc.reshape(local_rows, width).astype(jnp.bfloat16)
    middle = (
        hidden
        + jnp.dot(ctx_low, wo_full, preferred_element_type=jnp.float32)
        + bo_full.astype(jnp.float32)
    )
    normed_two, factor_two = normalize(middle)
    norm_two = (normed_two * gb_full.astype(jnp.float32) + sb_full.astype(jnp.float32)).astype(
        jnp.bfloat16
    )
    pre_act = jnp.dot(norm_two, wu_full, preferred_element_type=jnp.float32) + bu_full.astype(
        jnp.float32
    )
    cdf_part = 0.5 * (1.0 + jax.scipy.special.erf(pre_act * 0.7071067811865476))
    act_low = (pre_act * cdf_part).astype(jnp.bfloat16)
    layer_out = (
        middle
        + jnp.dot(act_low, wd_full, preferred_element_type=jnp.float32)
        + bd_full.astype(jnp.float32)
    ).astype(jnp.bfloat16)
    regathered = (
        lax.all_gather(shards[0], ("seq", "batch"), axis=0, tiled=True),
        lax.all_gather(shards[1], ("seq", "batch"), axis=0, tiled=True),
        lax.all_gather(shards[2], ("seq", "batch"), axis=0, tiled=True),
        lax.all_gather(shards[3], ("seq", "batch"), axis=0, tiled=True),
        lax.all_gather(shards[4], ("seq", "batch"), axis=0, tiled=True),
        lax.all_gather(shards[5], ("seq", "batch"), axis=0, tiled=True),
        lax.all_gather(shards[6], ("seq", "batch"), axis=0, tiled=True),
        lax.all_gather(shards[7], ("seq", "batch"), axis=0, tiled=True),
        lax.all_gather(shards[8], ("seq", "batch"), axis=0, tiled=True),
        lax.all_gather(shards[9], ("seq", "batch"), axis=0, tiled=True),
        lax.all_gather(shards[10], ("seq", "batch"), axis=0, tiled=True),
        lax.all_gather(shards[11], ("seq", "batch"), axis=0, tiled=True),
        lax.all_gather(shards[12], ("seq", "batch"), axis=0, tiled=True),
        lax.all_gather(shards[13], ("seq", "batch"), axis=0, tiled=True),
        lax.all_gather(shards[14], ("seq", "batch"), axis=0, tiled=True),
    )
    (
        ga_back,
        sa_back,
        wq_back,
        bq_back,
        wk_back,
        wv_back,
        bv_back,
        wo_back,
        bo_back,
        gb_back,
        sb_back,
        wu_back,
        bu_back,
        wd_back,
        bd_back,
    ) = regathered
    d_out = cotangent[0]
    grad_wd = over_rows(act_low, d_out)
    grad_bd = jnp.sum(d_out.astype(jnp.float32), axis=0)
    d_act = over_cols(d_out, wd_back)
    slope = cdf_part + pre_act * jnp.exp(-0.5 * pre_act * pre_act) * 0.3989422804014327
    d_pre = (d_act * slope).astype(jnp.bfloat16)
    grad_wu = over_rows(norm_two, d_pre)
    grad_bu = jnp.sum(d_pre.astype(jnp.float32), axis=0)
    d_norm_two = over_cols(d_pre, wu_back)
    d_mid_norm, grad_gb, grad_sb = norm_backward(d_norm_two, normed_two, factor_two, gb_back)
    d_middle = d_out.astype(jnp.float32) + d_mid_norm
    d_branch = d_middle.astype(jnp.bfloat16)
    grad_wo = over_rows(ctx_low, d_branch)
    grad_bo = jnp.sum(d_branch.astype(jnp.float32), axis=0)
    d_ctx = over_cols(d_branch, wo_back).astype(jnp.bfloat16)
    do_heads = d_ctx.reshape(local_rows, heads, HD)
    delta = jnp.sum(d_ctx.astype(jnp.float32).reshape(local_rows, heads, HD) * ctx_acc, axis=-1).T
    k_back, v_back = (k_blocks, v_blocks)
    zero_heads = jnp.zeros((local_rows, heads, HD), jnp.float32)

    def grad_step(acc, item):
        k_part, v_part, index = item
        col_ids = index * block_rows + jnp.arange(block_rows, dtype=jnp.int32)

        def work(current):
            prob_low, d_score = grad_terms(
                q_heads, do_heads, lse, delta, k_part, v_part, row_ids, col_ids, prefix
            )
            current = current + 0.125 * jnp.einsum(
                "hqk,khd->qhd", d_score, k_part, preferred_element_type=jnp.float32
            )
            d_key = 0.125 * jnp.einsum(
                "hqk,qhd->khd", d_score, q_heads, preferred_element_type=jnp.float32
            )
            d_value = jnp.einsum(
                "hqk,qhd->khd", prob_low, do_heads, preferred_element_type=jnp.float32
            )
            return (current, (d_key, d_value))

        def skip(current):
            empty = jnp.zeros((block_rows, heads, HD), jnp.float32)
            return (current, (empty, empty))

        needed = (index * block_rows <= last_row) | (index * block_rows < prefix)
        return lax.cond(needed, work, skip, acc)

    dq_acc, (dk_blocks, dv_blocks) = lax.scan(grad_step, zero_heads, (k_back, v_back, block_ids))
    dk_local, dv_local = (
        lax.psum_scatter(
            dk_blocks.reshape(length, width).astype(jnp.bfloat16),
            "seq",
            scatter_dimension=0,
            tiled=True,
        ).astype(jnp.float32),
        lax.psum_scatter(
            dv_blocks.reshape(length, width).astype(jnp.bfloat16),
            "seq",
            scatter_dimension=0,
            tiled=True,
        ).astype(jnp.float32),
    )
    dq_low = dq_acc.reshape(local_rows, width).astype(jnp.bfloat16)
    dk_low = dk_local.astype(jnp.bfloat16)
    dv_low = dv_local.astype(jnp.bfloat16)
    grad_wq = over_rows(norm_one, dq_low)
    grad_bq = jnp.sum(dq_low.astype(jnp.float32), axis=0)
    grad_wk = over_rows(norm_one, dk_low)
    grad_wv = over_rows(norm_one, dv_low)
    grad_bv = jnp.sum(dv_low.astype(jnp.float32), axis=0)
    d_norm_one = (
        over_cols(dq_low, wq_back) + over_cols(dk_low, wk_back) + over_cols(dv_low, wv_back)
    )
    d_in_norm, grad_ga, grad_sa = norm_backward(d_norm_one, normed_one, factor_one, ga_back)
    grad_tokens = d_middle + d_in_norm
    summed = (
        lax.psum_scatter(grad_ga, ("seq", "batch"), scatter_dimension=0, tiled=True),
        lax.psum_scatter(grad_sa, ("seq", "batch"), scatter_dimension=0, tiled=True),
        lax.psum_scatter(grad_wq, ("seq", "batch"), scatter_dimension=0, tiled=True),
        lax.psum_scatter(grad_bq, ("seq", "batch"), scatter_dimension=0, tiled=True),
        lax.psum_scatter(grad_wk, ("seq", "batch"), scatter_dimension=0, tiled=True),
        lax.psum_scatter(grad_wv, ("seq", "batch"), scatter_dimension=0, tiled=True),
        lax.psum_scatter(grad_bv, ("seq", "batch"), scatter_dimension=0, tiled=True),
        lax.psum_scatter(grad_wo, ("seq", "batch"), scatter_dimension=0, tiled=True),
        lax.psum_scatter(grad_bo, ("seq", "batch"), scatter_dimension=0, tiled=True),
        lax.psum_scatter(grad_gb, ("seq", "batch"), scatter_dimension=0, tiled=True),
        lax.psum_scatter(grad_sb, ("seq", "batch"), scatter_dimension=0, tiled=True),
        lax.psum_scatter(grad_wu, ("seq", "batch"), scatter_dimension=0, tiled=True),
        lax.psum_scatter(grad_bu, ("seq", "batch"), scatter_dimension=0, tiled=True),
        lax.psum_scatter(grad_wd, ("seq", "batch"), scatter_dimension=0, tiled=True),
        lax.psum_scatter(grad_bd, ("seq", "batch"), scatter_dimension=0, tiled=True),
    )
    return (
        layer_out[None],
        grad_tokens[None],
        summed[0],
        summed[1],
        summed[2],
        summed[3],
        summed[4],
        summed[5],
        summed[6],
        summed[7],
        summed[8],
        summed[9],
        summed[10],
        summed[11],
        summed[12],
        summed[13],
        summed[14],
    )


def solution(mesh):
    placed = (
        P("batch", "seq", None),
        P("batch", "seq", None),
        P("batch"),
        P(("seq", "batch")),
        P(("seq", "batch")),
        P(("seq", "batch"), None),
        P(("seq", "batch")),
        P(("seq", "batch"), None),
        P(("seq", "batch"), None),
        P(("seq", "batch")),
        P(("seq", "batch"), None),
        P(("seq", "batch")),
        P(("seq", "batch")),
        P(("seq", "batch")),
        P(("seq", "batch"), None),
        P(("seq", "batch")),
        P(("seq", "batch"), None),
        P(("seq", "batch")),
    )
    return jax.shard_map(
        body,
        mesh=mesh,
        in_specs=placed,
        out_specs=(
            P("batch", "seq", None),
            P("batch", "seq", None),
            P(("seq", "batch")),
            P(("seq", "batch")),
            P(("seq", "batch"), None),
            P(("seq", "batch")),
            P(("seq", "batch"), None),
            P(("seq", "batch"), None),
            P(("seq", "batch")),
            P(("seq", "batch"), None),
            P(("seq", "batch")),
            P(("seq", "batch")),
            P(("seq", "batch")),
            P(("seq", "batch"), None),
            P(("seq", "batch")),
            P(("seq", "batch"), None),
            P(("seq", "batch")),
        ),
        check_vma=False,
    )
```

profile of v0, /device:TPU:0, one launch (start us, length us, event | category | flops | bytes accessed | tf_op | source)
XLA Modules:
  0.0 1545.5 jit_solution(5383057277159908306)
XLA Ops:
  17.0 42.6 %all-reduce.19 = (bf16[768]{0:T(1024)(128)(2,1)S(1)}, bf16[768]{0:T(1024)(128)(2,1)S(1)}, bf16[768]{0:T(1024)(128)(2,1)S(1)}, bf16[768]{0:T(1024)(128)(2,1)S(1)}...) all-reduce(bf16[768]{0:T(1024)(128)(2,1)S(1)} %dynamic-update-slice, ...), channel_id=1, replica_groups=mesh['seq'=16,'batch'=2] {'seq','batch'}, use_global_device_ids=true, to_apply=%add.1 | all-reduce | flops 9216 | bytes 36864
  61.9 6.2 all-gather.15.cloned.1.call-done
  68.1 2.4 fusion.68
  70.6 53.2 %all-gather.9.cloned.1.call-done = bf16[768,768]{1,0:T(8,128)(2,1)} async-done(((bf16[24,768]{1,0:T(8,128)(2,1)}), bf16[768,768]{1,0:T(8,128)(2,1)}) %all-gather.9.cloned.1.call-update) | async-done | bytes 1179664 | tf_op jit(solution)/shard_map/all_gather | solution.py:99
  123.8 2.4 convolution_convert_fusion.1
  130.1 49.6 %all-gather.13.cloned.1.call-done = bf16[768,768]{1,0:T(8,128)(2,1)} async-done(((bf16[24,768]{1,0:T(8,128)(2,1)}), bf16[768,768]{1,0:T(8,128)(2,1)}) %all-gather.13.cloned.1.call-update) | async-done | bytes 1179664 | tf_op jit(solution)/shard_map/all_gather | solution.py:97
  181.5 68.5 %all-gather.17.cloned.1.call-done = bf16[2048,768]{1,0:T(8,128)(2,1)} async-done(((bf16[128,768]{1,0:T(8,128)(2,1)}), bf16[2048,768]{1,0:T(8,128)(2,1)}) %all-gather.17.cloned.1.call-update) | async-done | bytes 3145744 | tf_op jit(solution)/shard_map/all_gather | solution.py:153
  250.0 3.2 copy.68
  253.2 4.0 reshape.279
  257.2 4.2 copy.70
  261.4 58.4 %all-gather.11.cloned.1.call-done = bf16[2048,768]{1,0:T(8,128)(2,1)} async-done(((bf16[128,768]{1,0:T(8,128)(2,1)}), bf16[2048,768]{1,0:T(8,128)(2,1)}) %all-gather.11.cloned.1.call-update) | async-done | bytes 3145744 | tf_op jit(solution)/shard_map/all_gather | solution.py:152
  319.9 3.2 copy.65
  323.1 4.0 reshape.277
  327.1 4.4 copy.69
  331.4 11.3 while.45
  333.3 3.5 conditional.9
  342.8 11.4 while.46
  344.7 3.6 conditional.10
  345.6 2.7 fusion.17
  354.3 20.9 %all-gather.19.cloned.1.call-done = bf16[768,768]{1,0:T(8,128)(2,1)} async-done(((bf16[24,768]{1,0:T(8,128)(2,1)}), bf16[768,768]{1,0:T(8,128)(2,1)}) %all-gather.19.cloned.1.call-update) | async-done | bytes 1179664 | tf_op jit(solution)/shard_map/all_gather | solution.py:102
  377.2 63.5 %all-gather.21.cloned.1.call-done = bf16[768,3072]{1,0:T(8,128)(2,1)} async-done(((bf16[24,3072]{1,0:T(8,128)(2,1)}), bf16[768,3072]{1,0:T(8,128)(2,1)}) %all-gather.21.cloned.1.call-update) | async-done | bytes 4718608 | tf_op jit(solution)/shard_map/all_gather | solution.py:106
  440.7 3.2 convolution_add_fusion
  444.0 62.2 %all-gather.23.cloned.1.call-done = bf16[3072,768]{1,0:T(8,128)(2,1)} async-done(((bf16[96,768]{1,0:T(8,128)(2,1)}), bf16[3072,768]{1,0:T(8,128)(2,1)}) %all-gather.23.cloned.1.call-update) | async-done | bytes 4718608 | tf_op jit(solution)/shard_map/all_gather | solution.py:108
  506.1 4.9 convert_reduce_fusion
  511.1 2.3 multiply_reduce_fusion
  515.0 22.2 %while.47 = (s32[]{:T(128)}, f32[128,12,64]{0,2,1:T(8,128)S(1)}, bf16[4,512,12,64]{1,3,2,0:T(8,128)(2,1)}, bf16[4,512,12,64]{1,3,2,0:T(8,128)(2,1)}, s32[4]{0:T(...) while((s32[]{:T(128)}, f32[128,12,64]{0,2,1:T(8,128)S(1)}, ...), condition=%wide.region_20.21_spmd.clone, body=%wide.region_17.20_spmd.clone.sunk | while | flops 513868928 | bytes 23059832 | solution.py:300
  517.1 8.6 conditional.11
  519.9 2.5 fusion.29
  537.3 4.3 copy.75
  541.6 2.7 copy.85
  544.2 4.7 copy.82
  549.0 4.3 copy.74
  553.3 2.7 copy.84
  556.0 4.9 copy.80
  566.1 137.8 %reduce-scatter.27.cloned.1.call-done = bf16[128,768]{1,0:T(8,128)(2,1)} async-done(((bf16[2048,768]{1,0:T(8,128)(2,1)}), bf16[128,768]{1,0:T(8,128)(2,1)}) %reduce-scatter.27.cloned.1.call-update) | async-done | bytes 196624
  703.9 3.0 fusion.104
  707.0 131.5 %reduce-scatter.25.cloned.1.call-done = bf16[128,768]{1,0:T(8,128)(2,1)} async-done(((bf16[2048,768]{1,0:T(8,128)(2,1)}), bf16[128,768]{1,0:T(8,128)(2,1)}) %reduce-scatter.25.cloned.1.call-update) | async-done | bytes 196624
  838.5 2.9 fusion.106
  841.5 5.1 fusion.93
  847.3 6.3 fusion.103
  856.2 4.0 fusion.69
  864.4 41.3 %all-reduce.18 = (f32[768]{0:T(1024)S(1)}, f32[768]{0:T(1024)S(1)}, f32[768]{0:T(1024)S(1)}, f32[768]{0:T(1024)S(1)}, f32[768]{0:T(1024)S(1)}, /*index=5*/f32[76...) all-reduce(f32[768]{0:T(1024)S(1)} %get-tuple-element.633, ...), channel_id=4, replica_groups=mesh['seq'=16,'batch'=2] {'seq','batch'}, use_global_device_ids=true, to_apply=%region_26.27.clone | all-reduce | flops 9216 | bytes 73728
  911.9 30.7 %reduce-scatter.19.cloned.1.call-done = f32[24,768]{1,0:T(8,128)} async-done(((f32[768,768]{1,0:T(8,128)}), f32[24,768]{1,0:T(8,128)}) %reduce-scatter.19.cloned.1.call-update) | async-done | bytes 73744 | tf_op jit(solution)/shard_map/reduce_scatter | solution.py:336
  942.6 104.6 %reduce-scatter.13.cloned.1.call-done = f32[24,768]{1,0:T(8,128)} async-done(((f32[768,768]{1,0:T(8,128)}), f32[24,768]{1,0:T(8,128)}) %reduce-scatter.13.cloned.1.call-update) | async-done | bytes 73744 | tf_op jit(solution)/shard_map/reduce_scatter | solution.py:331
  1047.3 103.9 %reduce-scatter.17.cloned.1.call-done = f32[24,768]{1,0:T(8,128)} async-done(((f32[768,768]{1,0:T(8,128)}), f32[24,768]{1,0:T(8,128)}) %reduce-scatter.17.cloned.1.call-update) | async-done | bytes 73744 | tf_op jit(solution)/shard_map/reduce_scatter | solution.py:334
  1151.2 104.6 %reduce-scatter.15.cloned.1.call-done = f32[24,768]{1,0:T(8,128)} async-done(((f32[768,768]{1,0:T(8,128)}), f32[24,768]{1,0:T(8,128)}) %reduce-scatter.15.cloned.1.call-update) | async-done | bytes 73744 | tf_op jit(solution)/shard_map/reduce_scatter | solution.py:333
  1255.8 141.0 %reduce-scatter.23.cloned.1.call-done = f32[96,768]{1,0:T(8,128)} async-done(((f32[3072,768]{1,0:T(8,128)}), f32[96,768]{1,0:T(8,128)}) %reduce-scatter.23.cloned.1.call-update) | async-done | bytes 294928 | tf_op jit(solution)/shard_map/reduce_scatter | solution.py:342
  1396.8 141.9 %reduce-scatter.21.cloned.1.call-done = f32[24,3072]{1,0:T(8,128)} async-done(((f32[768,3072]{1,0:T(8,128)}), f32[24,3072]{1,0:T(8,128)}) %reduce-scatter.21.cloned.1.call-update) | async-done | bytes 294928 | tf_op jit(solution)/shard_map/reduce_scatter | solution.py:340
  (247 shorter events, 63.6 us)
Async XLA Ops:
  7.2 172.5 %copy-start.3 = (bf16[1,128,768]{2,1,0:T(8,128)(2,1)S(1)}, bf16[1,128,768]{2,1,0:T(8,128)(2,1)}, u32[]{:S(2)}) copy-start(bf16[1,128,768]{2,1,0:T(8,128)(2,1)} %param.30) | copy-start | bytes 589828
  7.2 60.9 %all-gather.15.cloned.1.call-start = ((), (), s32[]{:S(2)}) async-start(), calls=%async_computation.11 | async-start | bytes 1216512 | tf_op jit(solution)/shard_map/all_gather | solution.py:100
  7.9 115.9 %all-gather.9.cloned.1.call-start = ((), (), s32[]{:S(2)}) async-start(), calls=%async_computation.8 | async-start | bytes 1216512 | tf_op jit(solution)/shard_map/all_gather | solution.py:99
  8.7 171.0 %all-gather.13.cloned.1.call-start = ((), (), s32[]{:S(2)}) async-start(), calls=%async_computation.10 | async-start | bytes 1216512 | tf_op jit(solution)/shard_map/all_gather | solution.py:97
  9.4 240.6 %all-gather.17.cloned.1.call-start = ((), (), s32[]{:S(2)}) async-start(), calls=%async_computation.12 | async-start | bytes 3342336 | tf_op jit(solution)/shard_map/all_gather | solution.py:153
  60.7 119.0 %copy-start.16 = (f32[128]{0:T(128)}, f32[128]{0:T(128)S(1)}, u32[]{:S(2)}) copy-start(f32[128]{0:T(128)S(1)} %broadcast_multiply_fusion.5) | copy-start | bytes 1540
  61.9 117.8 %copy-start.27 = (f32[128]{0:T(128)}, f32[128]{0:T(128)S(1)}, u32[]{:S(2)}) copy-start(f32[128]{0:T(128)S(1)} %add_rsqrt_fusion.1) | copy-start | bytes 1540
  70.5 249.3 %all-gather.11.cloned.1.call-start = ((), (), s32[]{:S(2)}) async-start(), calls=%async_computation.9 | async-start | bytes 3342336 | tf_op jit(solution)/shard_map/all_gather | solution.py:152
  126.3 249.0 %all-gather.19.cloned.1.call-start = ((), (), s32[]{:S(2)}) async-start(), calls=%async_computation.13 | async-start | bytes 1216512 | tf_op jit(solution)/shard_map/all_gather | solution.py:102
  126.8 313.9 %all-gather.21.cloned.1.call-start = ((), (), s32[]{:S(2)}) async-start(), calls=%async_computation.14 | async-start | bytes 4866048 | tf_op jit(solution)/shard_map/all_gather | solution.py:106
  127.6 378.5 %all-gather.23.cloned.1.call-start = ((), (), s32[]{:S(2)}) async-start(), calls=%async_computation.15 | async-start | bytes 4866048 | tf_op jit(solution)/shard_map/all_gather | solution.py:108
  128.3 575.6 %reduce-scatter.27.cloned.1.call-start = ((), (), s32[]{:S(2)}) async-start(), calls=%async_computation.23 | async-start | bytes 3342336
  342.8 32.4 %copy-start.19 = (f32[768]{0:T(1024)S(1)}, f32[768]{0:T(1024)}, u32[]{:S(2)}) copy-start(f32[768]{0:T(1024)} %convert_element_type.155) | copy-start | bytes 9220
  342.8 97.9 %copy-start.12 = (f32[3072]{0:T(1024)S(1)}, f32[3072]{0:T(1024)}, u32[]{:S(2)}) copy-start(f32[3072]{0:T(1024)} %convert_element_type.159) | copy-start | bytes 36868
  354.3 21.0 %copy-start.31 = (f32[12,128]{1,0:T(8,128)}, f32[12,128]{1,0:T(8,128)S(1)}, u32[]{:S(2)}) copy-start(f32[12,128]{1,0:T(8,128)S(1)} %get-tuple-element.1153) | copy-start | bytes 18436
  354.3 89.6 %copy-start.6 = (bf16[128,12,64]{0,2,1:T(8,128)(2,1)}, bf16[128,12,64]{0,2,1:T(8,128)(2,1)S(1)}, u32[]{:S(2)}) copy-start(bf16[128,12,64]{0,2,1:T(8,128)(2,1)S(1)} %convert_element_type.153) | copy-start | bytes 589828
  377.0 67.0 %copy-start.13 = (f32[128]{0:T(128)}, f32[128]{0:T(128)S(1)}, u32[]{:S(2)}) copy-start(f32[128]{0:T(128)S(1)} %broadcast_multiply_fusion.4) | copy-start | bytes 1540
  377.2 66.8 %copy-start.24 = (f32[128]{0:T(128)}, f32[128]{0:T(128)S(1)}, u32[]{:S(2)}) copy-start(f32[128]{0:T(128)S(1)} %add_rsqrt_fusion) | copy-start | bytes 1540
  443.9 67.1 %copy-start = (f32[128,3072]{1,0:T(8,128)}, f32[128,3072]{1,0:T(8,128)S(1)}, u32[]{:S(2)}) copy-start(f32[128,3072]{1,0:T(8,128)S(1)} %convolution_add_fusion) | copy-start | bytes 4718596
  506.1 4.9 copy-start.2
  506.1 4.9 copy-start.14
  506.1 4.9 copy-start.25
  511.0 2.4 copy-start.5
  511.0 2.4 copy-start.9
  511.1 3.2 copy-start.4
  517.2 2.7 copy-start.32
  549.0 289.6 %reduce-scatter.25.cloned.1.call-start = ((), (), s32[]{:S(2)}) async-start(), calls=%async_computation.22 | async-start | bytes 3342336
  560.9 0.9 copy-start.7
  560.9 3.0 copy-start.17
  560.9 3.0 copy-start.28
  560.9 381.7 %reduce-scatter.19.cloned.1.call-start = ((), (), s32[]{:S(2)}) async-start(), calls=%async_computation.19 | async-start | bytes 2433024 | tf_op jit(solution)/shard_map/reduce_scatter | solution.py:336
  563.7 483.6 %reduce-scatter.13.cloned.1.call-start = ((), (), s32[]{:S(2)}) async-start(), calls=%async_computation.16 | async-start | bytes 2433024 | tf_op jit(solution)/shard_map/reduce_scatter | solution.py:331
  566.0 585.2 %reduce-scatter.17.cloned.1.call-start = ((), (), s32[]{:S(2)}) async-start(), calls=%async_computation.18 | async-start | bytes 2433024 | tf_op jit(solution)/shard_map/reduce_scatter | solution.py:334
  707.0 134.5 %copy-start.1 = (f32[128,3072]{1,0:T(8,128)S(1)}, f32[128,3072]{1,0:T(8,128)}, u32[]{:S(2)}) copy-start(f32[128,3072]{1,0:T(8,128)} %copy-done) | copy-start | bytes 4718596
  707.0 134.5 %copy-start.10 = (bf16[1,128,768]{2,1,0:T(8,128)(2,1)S(1)}, bf16[1,128,768]{2,1,0:T(8,128)(2,1)}, u32[]{:S(2)}) copy-start(bf16[1,128,768]{2,1,0:T(8,128)(2,1)} %param.31) | copy-start | bytes 589828
  707.0 548.9 %reduce-scatter.15.cloned.1.call-start = ((), (), s32[]{:S(2)}) async-start(), calls=%async_computation.17 | async-start | bytes 2433024 | tf_op jit(solution)/shard_map/reduce_scatter | solution.py:333
  841.4 555.4 %reduce-scatter.23.cloned.1.call-start = ((), (), s32[]{:S(2)}) async-start(), calls=%async_computation.21 | async-start | bytes 9732096 | tf_op jit(solution)/shard_map/reduce_scatter | solution.py:342
  846.6 692.1 %reduce-scatter.21.cloned.1.call-start = ((), (), s32[]{:S(2)}) async-start(), calls=%async_computation.20 | async-start | bytes 9732096 | tf_op jit(solution)/shard_map/reduce_scatter | solution.py:340
  853.5 0.7 copy-start.33
  856.1 4.1 copy-start.8
  856.1 4.4 copy-start.11
  856.1 6.3 copy-start.18
  856.2 6.2 copy-start.29
  860.2 4.1 copy-start.20
  860.2 4.2 copy-start.21
  860.2 4.2 copy-start.22
  860.2 4.2 copy-start.23
  860.2 4.2 copy-start.30
  (2 other events, 1.3 us)
Sparse Core Ops, SparseCore 0:
  10.9 57.0 all-gather.14
  71.0 52.7 all-gather.8
  126.7 52.9 all-gather.12
  182.9 67.0 all-gather.16
  253.2 66.6 all-gather.10
  322.6 52.5 all-gather.18
  378.1 62.5 all-gather.20
  443.6 62.4 all-gather.22
  549.1 154.7 reduce-scatter.26
  708.7 129.7 reduce-scatter.24
  844.4 98.2 reduce-scatter.18
  949.2 98.0 reduce-scatter.12
  1053.1 98.0 reduce-scatter.16
  1157.8 98.0 reduce-scatter.14
  1262.2 134.5 reduce-scatter.22
  1404.1 134.4 reduce-scatter.20
where the time goes:
time: 1550 us
  waiting for transfers between devices  1280 us (83%)
  blocking collectives  84 us (5%)
  local copies, waits for them, and re-layouts  74.9 us (5%)
  matrix products  62.4 us (4%)
  loops' own time  16.7 us (1%)
    unnamed x18, waiting for transfers between devices  273 us
    reduce_scatter x1, waiting for transfers between devices, body(): lax.psum_scatter(grad_wu, ('seq', 'batch'), scatter_dimension=0, tiled=True)  142 us
    reduce_scatter x1, waiting for transfers between devices, body(): lax.psum_scatter(grad_wd, ('seq', 'batch'), scatter_dimension=0, tiled=True)  141 us
    reduce_scatter x1, waiting for transfers between devices, body(): lax.psum_scatter(grad_wk, ('seq', 'batch'), scatter_dimension=0, tiled=True)  105 us
    reduce_scatter x1, waiting for transfers between devices, body(): lax.psum_scatter(grad_wq, ('seq', 'batch'), scatter_dimension=0, tiled=True)  105 us
    reduce_scatter x1, waiting for transfers between devices, body(): lax.psum_scatter(grad_wv, ('seq', 'batch'), scatter_dimension=0, tiled=True)  104 us
    unnamed x2, blocking collectives  84 us
    all_gather x1, waiting for transfers between devices, body(): lax.all_gather(v_low, 'seq', axis=0, tiled=True)  68.5 us
  transfers between devices with their start and end apart: 16, of which 16 were waited for; matrix products, arithmetic and copies ran while one was open for 7% of the time, Pallas kernels for 0%

commit v1 on v0

--- a/solution.py
+++ b/solution.py
@@ -5,6 +5,28 @@
 
 HD = 64
 EPS = 1e-05
+
+
+def in_order(blocks, dim):
+    blocks = jnp.moveaxis(blocks, 0, dim)
+    shape = blocks.shape
+    return blocks.reshape(*shape[:dim], shape[dim] * shape[dim + 1], *shape[dim + 2 :])
+
+
+def gather_around(value, axis, dim):
+    length = lax.axis_size(axis)
+    pairs = [(i, (i + 1) % length) for i in range(length)]
+    back = [(b, a) for a, b in pairs]
+    lower, upper = ([], [])
+    for hop in range(length - 1):
+        if hop % 2 == 0:
+            lower.append(lax.ppermute(lower[-1] if lower else value, axis, pairs))
+        else:
+            upper.append(lax.ppermute(upper[-1] if upper else value, axis, back))
+    blocks = jnp.stack([*lower[::-1], value, *upper])
+    shift = lax.axis_index(axis) - len(lower)
+    blocks = blocks[(jnp.arange(length) - shift) % length]
+    return in_order(blocks, dim)
 
 
 def normalize(values):
@@ -149,7 +171,7 @@
         jnp.dot(norm_one, wv_full, preferred_element_type=jnp.float32) + bv_full.astype(jnp.float32)
     ).astype(jnp.bfloat16)
     k_all, v_all = (
-        lax.all_gather(k_low, "seq", axis=0, tiled=True),
+        gather_around(k_low, "seq", 0),
         lax.all_gather(v_low, "seq", axis=0, tiled=True),
     )
     q_heads = q_low.reshape(local_rows, heads, HD)

time: 1550 us -> 1500 us (0.968)
  waiting for transfers between devices: 1280 us -> 1170 us
  starting transfers between devices: 1.11 us -> 45.9 us
    all_gather x1 -> x0, waiting for transfers between devices: 58.4 us -> none  [body(): lax.all_gather(k_low, 'seq', axis=0, tiled=True)]
    all_gather x1, waiting for transfers between devices: 68.5 us -> 11.4 us  [body(): lax.all_gather(v_low, 'seq', axis=0, tiled=True)]
    all_gather x1, waiting for transfers between devices: 49.6 us -> 0.01 us  [body(): lax.all_gather(shards[2], ('seq', 'batch'), axis=0, tiled=True)]
    ppermute x0 -> x15, starting transfers between devices: none -> 45.3 us  [the longest x7 30.9 us: gather_around(): upper.append(lax.ppermute(upper[-1] if upper else value, axis, back))]
    ppermute x0 -> x15, waiting for transfers between devices: none -> 41.2 us  [the longest x8 41.2 us: gather_around(): lower.append(lax.ppermute(lower[-1] if lower else value, axis, pairs))]
    unnamed x100 -> x115, local copies, waits for them, and re-layouts: 38.7 us -> 47.2 us
    unnamed x18 -> x17, waiting for transfers between devices: 273 us -> 273 us
  transfers between devices with their start and end apart: 16 -> 30, of which waited for: 16 -> 22; matrix products, arithmetic and copies ran while one was open for 7% -> 8% of each run, Pallas kernels for 0% -> 0%
where the time goes in v1:
time: 1500 us; the launch traced here: 1490 us
  waiting for transfers between devices  1170 us (78%)
  local copies, waits for them, and re-layouts  87.1 us (6%)
  blocking collectives  83.8 us (6%)
  matrix products  61.7 us (4%)
  starting transfers between devices  45.9 us (3%)
  loops' own time  16.7 us (1%)
    unnamed x17, waiting for transfers between devices  273 us
    reduce_scatter x1, waiting for transfers between devices, body(): lax.psum_scatter(grad_wu, ('seq', 'batch'), scatter_dimension=0, tiled=True)  142 us
    reduce_scatter x1, waiting for transfers between devices, body(): lax.psum_scatter(grad_wd, ('seq', 'batch'), scatter_dimension=0, tiled=True)  141 us
    reduce_scatter x1, waiting for transfers between devices, body(): lax.psum_scatter(grad_wq, ('seq', 'batch'), scatter_dimension=0, tiled=True)  105 us
    reduce_scatter x1, waiting for transfers between devices, body(): lax.psum_scatter(grad_wk, ('seq', 'batch'), scatter_dimension=0, tiled=True)  105 us
    reduce_scatter x1, waiting for transfers between devices, body(): lax.psum_scatter(grad_wv, ('seq', 'batch'), scatter_dimension=0, tiled=True)  104 us
    unnamed x2, blocking collectives  83.8 us
    all_gather x1, waiting for transfers between devices, body(): lax.all_gather(shards[11], ('seq', 'batch'), axis=0, tiled=True)  63.4 us
  transfers between devices with their start and end apart: 30, of which 22 were waited for; matrix products, arithmetic and copies ran while one was open for 8% of the time, Pallas kernels for 0%

profile of v1, /device:TPU:0, one launch (start us, length us, event | category | flops | bytes accessed | tf_op | source)
XLA Modules:
  0.0 1488.3 jit_solution(7233281467565956108)
XLA Ops:
  17.0 42.6 %all-reduce.19 = (bf16[768]{0:T(1024)(128)(2,1)S(1)}, bf16[768]{0:T(1024)(128)(2,1)S(1)}, bf16[768]{0:T(1024)(128)(2,1)S(1)}, bf16[768]{0:T(1024)(128)(2,1)S(1)}...) all-reduce(bf16[768]{0:T(1024)(128)(2,1)S(1)} %dynamic-update-slice, ...), channel_id=1, replica_groups=mesh['seq'=16,'batch'=2] {'seq','batch'}, use_global_device_ids=true, to_apply=%add.1 | all-reduce | flops 9216 | bytes 36864
  61.8 6.3 all-gather.12.cloned.1.call-done
  72.5 51.3 %all-gather.8.cloned.1.call-done = bf16[768,768]{1,0:T(8,128)(2,1)} async-done(((bf16[24,768]{1,0:T(8,128)(2,1)}), bf16[768,768]{1,0:T(8,128)(2,1)}) %all-gather.8.cloned.1.call-update) | async-done | bytes 1179664 | tf_op jit(solution)/shard_map/all_gather | solution.py:121
  127.1 9.2 collective-permute-done
  136.3 5.6 collective-permute-start.8
  141.9 4.7 collective-permute-done.1
  147.1 5.4 collective-permute-start.9
  152.5 4.3 collective-permute-done.2
  159.3 5.3 collective-permute-start.10
  164.6 3.2 collective-permute-done.3
  170.3 4.7 collective-permute-start.11
  175.0 6.2 collective-permute-done.4
  188.0 4.8 collective-permute-done.5
  199.0 6.4 collective-permute-done.6
  209.7 3.7 collective-permute-start.14
  229.6 3.5 copy.65
  233.1 4.0 reshape_reshape.3
  239.5 11.3 while.45
  241.4 3.5 conditional.9
  251.4 11.4 all-gather.14.cloned.1.call-done
  262.7 3.2 copy.68
  265.9 4.0 reshape.324
  270.0 4.4 copy.70
  274.4 11.4 while.46
  276.3 3.6 conditional.10
  285.9 32.2 %all-gather.16.cloned.1.call-done = bf16[768,768]{1,0:T(8,128)(2,1)} async-done(((bf16[24,768]{1,0:T(8,128)(2,1)}), bf16[768,768]{1,0:T(8,128)(2,1)}) %all-gather.16.cloned.1.call-update) | async-done | bytes 1179664 | tf_op jit(solution)/shard_map/all_gather | solution.py:124
  320.0 63.4 %all-gather.18.cloned.1.call-done = bf16[768,3072]{1,0:T(8,128)(2,1)} async-done(((bf16[24,3072]{1,0:T(8,128)(2,1)}), bf16[768,3072]{1,0:T(8,128)(2,1)}) %all-gather.18.cloned.1.call-update) | async-done | bytes 4718608 | tf_op jit(solution)/shard_map/all_gather | solution.py:128
  383.4 3.2 convolution_add_fusion
  386.7 62.1 %all-gather.20.cloned.1.call-done = bf16[3072,768]{1,0:T(8,128)(2,1)} async-done(((bf16[96,768]{1,0:T(8,128)(2,1)}), bf16[3072,768]{1,0:T(8,128)(2,1)}) %all-gather.20.cloned.1.call-update) | async-done | bytes 4718608 | tf_op jit(solution)/shard_map/all_gather | solution.py:130
  448.8 4.9 convert_reduce_fusion
  457.7 22.2 %while.47 = (s32[]{:T(128)}, f32[128,12,64]{0,2,1:T(8,128)S(1)}, bf16[4,512,12,64]{1,3,2,0:T(8,128)(2,1)}, bf16[4,512,12,64]{1,3,2,0:T(8,128)(2,1)}, s32[4]{0:T(...) while((s32[]{:T(128)}, f32[128,12,64]{0,2,1:T(8,128)S(1)}, ...), condition=%wide.region_20.21_spmd.clone, body=%wide.region_17.20_spmd.clone.sunk | while | flops 513868928 | bytes 23059832 | solution.py:322
  459.8 8.6 conditional.11
  479.9 4.3 copy.75
  487.0 4.7 copy.82
  491.8 4.3 copy.74
  498.8 4.8 copy.80
  508.9 137.5 %reduce-scatter.27.cloned.1.call-done = bf16[128,768]{1,0:T(8,128)(2,1)} async-done(((bf16[2048,768]{1,0:T(8,128)(2,1)}), bf16[128,768]{1,0:T(8,128)(2,1)}) %reduce-scatter.27.cloned.1.call-update) | async-done | bytes 196624
  649.4 131.8 %reduce-scatter.25.cloned.1.call-done = bf16[128,768]{1,0:T(8,128)(2,1)} async-done(((bf16[2048,768]{1,0:T(8,128)(2,1)}), bf16[128,768]{1,0:T(8,128)(2,1)}) %reduce-scatter.25.cloned.1.call-update) | async-done | bytes 196624
  784.3 5.1 fusion.93
  790.0 6.3 fusion.105
  798.9 4.1 fusion.69
  807.1 41.3 %all-reduce.18 = (f32[768]{0:T(1024)S(1)}, f32[768]{0:T(1024)S(1)}, f32[768]{0:T(1024)S(1)}, f32[768]{0:T(1024)S(1)}, f32[768]{0:T(1024)S(1)}, /*index=5*/f32[76...) all-reduce(f32[768]{0:T(1024)S(1)} %get-tuple-element.633, ...), channel_id=4, replica_groups=mesh['seq'=16,'batch'=2] {'seq','batch'}, use_global_device_ids=true, to_apply=%region_26.27.clone | all-reduce | flops 9216 | bytes 73728
  854.6 30.7 %reduce-scatter.19.cloned.1.call-done = f32[24,768]{1,0:T(8,128)} async-done(((f32[768,768]{1,0:T(8,128)}), f32[24,768]{1,0:T(8,128)}) %reduce-scatter.19.cloned.1.call-update) | async-done | bytes 73744 | tf_op jit(solution)/shard_map/reduce_scatter | solution.py:358
  885.2 104.8 %reduce-scatter.13.cloned.1.call-done = f32[24,768]{1,0:T(8,128)} async-done(((f32[768,768]{1,0:T(8,128)}), f32[24,768]{1,0:T(8,128)}) %reduce-scatter.13.cloned.1.call-update) | async-done | bytes 73744 | tf_op jit(solution)/shard_map/reduce_scatter | solution.py:353
  990.0 103.8 %reduce-scatter.17.cloned.1.call-done = f32[24,768]{1,0:T(8,128)} async-done(((f32[768,768]{1,0:T(8,128)}), f32[24,768]{1,0:T(8,128)}) %reduce-scatter.17.cloned.1.call-update) | async-done | bytes 73744 | tf_op jit(solution)/shard_map/reduce_scatter | solution.py:356
  1093.8 104.8 %reduce-scatter.15.cloned.1.call-done = f32[24,768]{1,0:T(8,128)} async-done(((f32[768,768]{1,0:T(8,128)}), f32[24,768]{1,0:T(8,128)}) %reduce-scatter.15.cloned.1.call-update) | async-done | bytes 73744 | tf_op jit(solution)/shard_map/reduce_scatter | solution.py:355
  1198.6 141.0 %reduce-scatter.23.cloned.1.call-done = f32[96,768]{1,0:T(8,128)} async-done(((f32[3072,768]{1,0:T(8,128)}), f32[96,768]{1,0:T(8,128)}) %reduce-scatter.23.cloned.1.call-update) | async-done | bytes 294928 | tf_op jit(solution)/shard_map/reduce_scatter | solution.py:364
  1339.5 142.0 %reduce-scatter.21.cloned.1.call-done = f32[24,3072]{1,0:T(8,128)} async-done(((f32[768,3072]{1,0:T(8,128)}), f32[24,3072]{1,0:T(8,128)}) %reduce-scatter.21.cloned.1.call-update) | async-done | bytes 294928 | tf_op jit(solution)/shard_map/reduce_scatter | solution.py:362
  (293 shorter events, 126.5 us)
Async XLA Ops:
  7.2 200.7 %copy-start.3 = (bf16[1,128,768]{2,1,0:T(8,128)(2,1)S(1)}, bf16[1,128,768]{2,1,0:T(8,128)(2,1)}, u32[]{:S(2)}) copy-start(bf16[1,128,768]{2,1,0:T(8,128)(2,1)} %param.30) | copy-start | bytes 589828
  7.2 60.9 %all-gather.12.cloned.1.call-start = ((), (), s32[]{:S(2)}) async-start(), calls=%async_computation.10 | async-start | bytes 1216512 | tf_op jit(solution)/shard_map/all_gather | solution.py:122
  7.9 115.9 %all-gather.8.cloned.1.call-start = ((), (), s32[]{:S(2)}) async-start(), calls=%async_computation.8 | async-start | bytes 1216512 | tf_op jit(solution)/shard_map/all_gather | solution.py:121
  8.7 199.2 %all-gather.10.cloned.1.call-start = ((), (), s32[]{:S(2)}) async-start(), calls=%async_computation.9 | async-start | bytes 1216512 | tf_op jit(solution)/shard_map/all_gather | solution.py:119
  9.4 253.3 %all-gather.14.cloned.1.call-start = ((), (), s32[]{:S(2)}) async-start(), calls=%async_computation.11 | async-start | bytes 3342336 | tf_op jit(solution)/shard_map/all_gather | solution.py:175
  60.7 147.2 %copy-start.16 = (f32[128]{0:T(128)}, f32[128]{0:T(128)S(1)}, u32[]{:S(2)}) copy-start(f32[128]{0:T(128)S(1)} %broadcast_multiply_fusion.5) | copy-start | bytes 1540
  61.8 146.1 %copy-start.27 = (f32[128]{0:T(128)}, f32[128]{0:T(128)S(1)}, u32[]{:S(2)}) copy-start(f32[128]{0:T(128)S(1)} %add_rsqrt_fusion.1) | copy-start | bytes 1540
  70.5 247.5 %all-gather.16.cloned.1.call-start = ((), (), s32[]{:S(2)}) async-start(), calls=%async_computation.12 | async-start | bytes 1216512 | tf_op jit(solution)/shard_map/all_gather | solution.py:124
  71.1 312.3 %all-gather.18.cloned.1.call-start = ((), (), s32[]{:S(2)}) async-start(), calls=%async_computation.13 | async-start | bytes 4866048 | tf_op jit(solution)/shard_map/all_gather | solution.py:128
  71.7 377.1 %all-gather.20.cloned.1.call-start = ((), (), s32[]{:S(2)}) async-start(), calls=%async_computation.14 | async-start | bytes 4866048 | tf_op jit(solution)/shard_map/all_gather | solution.py:130
  72.5 573.9 %reduce-scatter.27.cloned.1.call-start = ((), (), s32[]{:S(2)}) async-start(), calls=%async_computation.22 | async-start | bytes 3342336
  125.6 10.7 collective-permute-start
  136.3 10.3 collective-permute-start.1
  136.3 10.8 collective-permute-start.8
  146.6 10.2 collective-permute-start.2
  147.1 12.3 collective-permute-start.9
  156.8 11.0 collective-permute-start.3
  159.3 11.0 collective-permute-start.10
  167.8 13.3 collective-permute-start.4
  170.3 14.6 collective-permute-start.11
  181.2 11.6 collective-permute-start.5
  184.9 11.0 collective-permute-start.12
  192.8 12.6 collective-permute-start.6
  195.9 13.8 collective-permute-start.13
  205.4 10.3 collective-permute-start.7
  209.7 16.4 %collective-permute-start.14 = (bf16[128,768]{1,0:T(8,128)(2,1)S(1)}, bf16[128,768]{1,0:T(8,128)(2,1)S(1)}, u32[]{:S(2)}, u32[]{:S(2)}) collective-permute-start(bf16[128,768]{1,0:T(8,128)(2,1)S(1)} %collective-permute-done.13), channel_id=1, source_target_pairs={{2,0},{4,2},{6,4},{8,6},{10,8},{12,10},{14,12},{16,14},{18,16},{20... | collective-permute-start | bytes 589832 | tf_op jit(solution)/shard_map/ppermute | solution.py:25
  270.0 4.4 copy-start.31
  274.4 43.7 %copy-start.19 = (f32[768]{0:T(1024)S(1)}, f32[768]{0:T(1024)}, u32[]{:S(2)}) copy-start(f32[768]{0:T(1024)} %convert_element_type.155) | copy-start | bytes 9220
  274.4 109.1 %copy-start.12 = (f32[3072]{0:T(1024)S(1)}, f32[3072]{0:T(1024)}, u32[]{:S(2)}) copy-start(f32[3072]{0:T(1024)} %convert_element_type.159) | copy-start | bytes 36868
  285.9 100.8 %copy-start.6 = (bf16[128,12,64]{0,2,1:T(8,128)(2,1)}, bf16[128,12,64]{0,2,1:T(8,128)(2,1)S(1)}, u32[]{:S(2)}) copy-start(bf16[128,12,64]{0,2,1:T(8,128)(2,1)S(1)} %convert_element_type.153) | copy-start | bytes 589828
  319.8 66.8 %copy-start.13 = (f32[128]{0:T(128)}, f32[128]{0:T(128)S(1)}, u32[]{:S(2)}) copy-start(f32[128]{0:T(128)S(1)} %broadcast_multiply_fusion.4) | copy-start | bytes 1540
  320.0 66.6 %copy-start.24 = (f32[128]{0:T(128)}, f32[128]{0:T(128)S(1)}, u32[]{:S(2)}) copy-start(f32[128]{0:T(128)S(1)} %add_rsqrt_fusion) | copy-start | bytes 1540
  386.7 67.1 %copy-start = (f32[128,3072]{1,0:T(8,128)}, f32[128,3072]{1,0:T(8,128)S(1)}, u32[]{:S(2)}) copy-start(f32[128,3072]{1,0:T(8,128)S(1)} %convolution_add_fusion) | copy-start | bytes 4718596
  448.8 4.9 copy-start.2
  448.8 4.9 copy-start.14
  448.8 4.9 copy-start.25
  491.7 289.5 %reduce-scatter.25.cloned.1.call-start = ((), (), s32[]{:S(2)}) async-start(), calls=%async_computation.21 | async-start | bytes 3342336
  503.7 381.5 %reduce-scatter.19.cloned.1.call-start = ((), (), s32[]{:S(2)}) async-start(), calls=%async_computation.18 | async-start | bytes 2433024 | tf_op jit(solution)/shard_map/reduce_scatter | solution.py:358
  506.5 483.6 %reduce-scatter.13.cloned.1.call-start = ((), (), s32[]{:S(2)}) async-start(), calls=%async_computation.15 | async-start | bytes 2433024 | tf_op jit(solution)/shard_map/reduce_scatter | solution.py:353
  508.8 585.0 %reduce-scatter.17.cloned.1.call-start = ((), (), s32[]{:S(2)}) async-start(), calls=%async_computation.17 | async-start | bytes 2433024 | tf_op jit(solution)/shard_map/reduce_scatter | solution.py:356
  649.4 134.9 %copy-start.1 = (f32[128,3072]{1,0:T(8,128)S(1)}, f32[128,3072]{1,0:T(8,128)}, u32[]{:S(2)}) copy-start(f32[128,3072]{1,0:T(8,128)} %copy-done) | copy-start | bytes 4718596
  649.4 134.9 %copy-start.10 = (bf16[1,128,768]{2,1,0:T(8,128)(2,1)S(1)}, bf16[1,128,768]{2,1,0:T(8,128)(2,1)}, u32[]{:S(2)}) copy-start(bf16[1,128,768]{2,1,0:T(8,128)(2,1)} %param.31) | copy-start | bytes 589828
  649.4 549.2 %reduce-scatter.15.cloned.1.call-start = ((), (), s32[]{:S(2)}) async-start(), calls=%async_computation.16 | async-start | bytes 2433024 | tf_op jit(solution)/shard_map/reduce_scatter | solution.py:355
  784.2 555.3 %reduce-scatter.23.cloned.1.call-start = ((), (), s32[]{:S(2)}) async-start(), calls=%async_computation.20 | async-start | bytes 9732096 | tf_op jit(solution)/shard_map/reduce_scatter | solution.py:364
  789.4 692.2 %reduce-scatter.21.cloned.1.call-start = ((), (), s32[]{:S(2)}) async-start(), calls=%async_computation.19 | async-start | bytes 9732096 | tf_op jit(solution)/shard_map/reduce_scatter | solution.py:362
  798.8 4.4 copy-start.11
  798.8 6.3 copy-start.18
  798.9 6.3 copy-start.29
  (16 other events, 44.3 us)
Sparse Core Ops, SparseCore 0:
  10.9 57.0 all-gather.11
  71.0 52.7 all-gather.7
  126.7 60.2 all-gather.9
  190.2 72.4 all-gather.13
  265.5 52.5 all-gather.15
  320.8 62.5 all-gather.17
  386.3 62.4 all-gather.19
  491.8 154.4 reduce-scatter.26
  651.3 129.8 reduce-scatter.24
  787.0 98.2 reduce-scatter.18
  892.0 98.0 reduce-scatter.12
  995.7 97.9 reduce-scatter.16
  1100.5 98.0 reduce-scatter.14
  1204.9 134.5 reduce-scatter.22
  1346.9 134.6 reduce-scatter.20
